TPU v7x, 32 devices: a whole 2x2x4 slice. The times are simulated.
32 devices in a mesh: dp: 16 (over z, y, core), tensor: 2 (over x).
Axes of the slice: x: 2, y: 2, z: 4, core: 2. Of those that a mesh axis runs over, the one named last changes fastest.
Arguments:
- latents_in: bfloat16 [16, 1024, 1152], P('dp', 'tensor'), may hold values from -6 to 6
- steps: int32 [16], P('dp'), may hold values from 0 to 999
- labels: int32 [16], P('dp'), may hold values from 0 to 999
- class_table: bfloat16 [1000, 1152], P(None, 'tensor'), may hold values from -6 to 6
- w_ada: bfloat16 [1152, 6912], P('tensor', 'dp'), may hold values from -0.1875 to 0.1875
- w_qkv: bfloat16 [3, 1152, 1152], P(None, 'dp', 'tensor'), may hold values from -0.1875 to 0.1875
- w_proj: bfloat16 [1152, 1152], P('tensor', 'dp'), may hold values from -3 to 3
- w_fc1: bfloat16 [1152, 4608], P('dp', 'tensor'), may hold values from -0.1875 to 0.1875
- w_fc2: bfloat16 [4608, 1152], P('tensor', 'dp'), may hold values from -0.09375 to 0.09375
- cotangent: bfloat16 [16, 1024, 1152], P('dp', 'tensor'), may hold values from -6 to 6
Outputs:
- block_out: bfloat16 [16, 1024, 1152], P('dp', 'tensor')
- grad_latents: float32 [16, 1024, 1152], P('dp', 'tensor')
- grad_class_table: float32 [1000, 1152], P(None, 'tensor')
- grad_w_ada: float32 [1152, 6912], P('tensor', 'dp')
- grad_w_qkv: float32 [3, 1152, 1152], P(None, 'dp', 'tensor')
- grad_w_proj: float32 [1152, 1152], P('tensor', 'dp')
- grad_w_fc1: float32 [1152, 4608], P('dp', 'tensor')
- grad_w_fc2: float32 [4608, 1152], P('tensor', 'dp')
All inputs are finite; a program needn't handle non-finite values.
Results may differ from a plain program's by a relative error of at most 0.02.
Values may be sent and summed in bfloat16 or wider, within the bound.
A program may use at most 192 MiB of HBM per device.

v0:
```python
import functools
import math
import jax
import jax.numpy as jnp
from jax import lax
from jax.sharding import PartitionSpec as P

D = 1152
H = 16
norm_epsilon = 1e-06
gelu_factor = 0.7978845608028654
gelu_cubic = 0.044715


def norm_rows(rows):
    average = jnp.mean(rows, axis=-1, keepdims=True)
    centred = rows - average
    variance = jnp.mean(centred * centred, axis=-1, keepdims=True)
    inv_std = lax.rsqrt(variance + norm_epsilon)
    return (centred * inv_std, inv_std)


def norm_back(grad_normed, normed, inv_std):
    first = jnp.mean(grad_normed, axis=-1, keepdims=True)
    second = jnp.mean(grad_normed * normed, axis=-1, keepdims=True)
    return inv_std * (grad_normed - first - normed * second)


def gelu_value(pre):
    inner = gelu_factor * (pre + gelu_cubic * pre * pre * pre)
    return 0.5 * pre * (1.0 + jnp.tanh(inner))


def gelu_slope(pre):
    tangent = jnp.tanh(gelu_factor * (pre + gelu_cubic * pre * pre * pre))
    return 0.5 * (1.0 + tangent) + 0.5 * pre * (1.0 - tangent * tangent) * gelu_factor * (
        1.0 + 3.0 * gelu_cubic * pre * pre
    )


def silu_value(value):
    return value * jax.nn.sigmoid(value)


def silu_slope(value):
    sigma = jax.nn.sigmoid(value)
    return sigma * (1.0 + value * (1.0 - sigma))


def time_columns(steps_float, columns, width):
    half = width // 2
    index = jnp.where(columns < half, columns, columns - half).astype(jnp.float32)
    freqs = jnp.exp(-math.log(10000.0) * index / half)
    angles = steps_float[:, None] * freqs[None, :]
    return jnp.where(columns[None, :] < half, jnp.cos(angles), jnp.sin(angles))


def attend(queries, keys, values, score_scale):
    scores = (
        jnp.einsum("qhd,khd->hqk", queries, keys, preferred_element_type=jnp.float32) * score_scale
    )
    largest = jnp.max(scores, axis=-1, keepdims=True)
    log_total = largest + jnp.log(jnp.sum(jnp.exp(scores - largest), axis=-1, keepdims=True))
    probs = jnp.exp(scores - log_total).astype(jnp.bfloat16)
    mixed = jnp.einsum("hqk,khd->qhd", probs, values, preferred_element_type=jnp.float32)
    return (mixed.astype(jnp.bfloat16), log_total[:, :, 0])


def attend_back(queries, keys, values, mixed, grad_mixed, log_totals, score_scale):
    scores = (
        jnp.einsum("qhd,khd->hqk", queries, keys, preferred_element_type=jnp.float32) * score_scale
    )
    probs = jnp.exp(scores - log_totals[:, :, None])
    grad_values = jnp.einsum(
        "hqk,qhd->khd", probs.astype(jnp.bfloat16), grad_mixed, preferred_element_type=jnp.float32
    )
    grad_probs = jnp.einsum("qhd,khd->hqk", grad_mixed, values, preferred_element_type=jnp.float32)
    delta = jnp.sum(grad_mixed.astype(jnp.float32) * mixed.astype(jnp.float32), axis=-1)
    grad_scores = (
        probs * (grad_probs - jnp.swapaxes(delta, 0, 1)[:, :, None]) * score_scale
    ).astype(jnp.bfloat16)
    grad_queries = jnp.einsum("hqk,khd->qhd", grad_scores, keys, preferred_element_type=jnp.float32)
    grad_keys = jnp.einsum("hqk,qhd->khd", grad_scores, queries, preferred_element_type=jnp.float32)
    return (grad_queries, grad_keys, grad_values)


def from_rank(value, ranks, step):
    return lax.ppermute(value, "tensor", [(i, (i - step) % ranks) for i in range(ranks)])


def fetch_rest(rows, ranks):
    got = [from_rank(rows, ranks, step) for step in range(1, ranks)]
    return got[0] if ranks == 2 else jnp.concatenate(got, axis=0)


def return_rest(partial, ranks):
    size = partial.shape[0] // (ranks - 1)
    total = None
    for step in range(1, ranks):
        part = partial[(step - 1) * size : step * size].astype(jnp.bfloat16)
        part = from_rank(part, ranks, ranks - step).astype(jnp.float32)
        total = part if total is None else total + part
    return total


def sum_ranks(value, ranks):
    total = value
    for step in range(1, ranks):
        total = total + from_rank(value, ranks, step)
    return total


def dot(spec, left, right):
    return jnp.einsum(spec, left, right, preferred_element_type=jnp.float32)


def join(own, rest):
    return jnp.concatenate([own, rest], axis=0)


def shards(
    ranks, latents_in, steps, labels, class_table, w_ada, w_qkv, w_proj, w_fc1, w_fc2, cotangent
):
    half = jnp.bfloat16
    rank = lax.axis_index("tensor")
    width = latents_in.shape[2]
    mine = latents_in.shape[1]
    owned = class_table.shape[1]
    head_size = D // H
    heads_here = owned // head_size
    score_scale = head_size ** (-0.5)
    highest = lax.Precision.HIGHEST
    marks = lax.all_gather(jnp.stack([steps, labels], axis=1), "dp", axis=0, tiled=True)
    all_steps, all_labels = (marks[:, 0], marks[:, 1])
    attn_w = lax.all_gather(
        jnp.concatenate([w_qkv[0], w_qkv[1], w_qkv[2], w_proj.T], axis=1), "dp", axis=0, tiled=True
    )
    mlp_w = lax.all_gather(jnp.concatenate([w_fc1, w_fc2.T], axis=1), "dp", axis=0, tiled=True)
    qkv_full, proj_t = (attn_w[:, : 3 * owned], attn_w[:, 3 * owned :])
    fc1_full, fc2_t = (mlp_w[:, : w_fc1.shape[1]], mlp_w[:, w_fc1.shape[1] :])
    columns = rank * owned + jnp.arange(owned, dtype=jnp.int32)
    classes = jnp.arange(class_table.shape[0], dtype=jnp.int32)
    one_hot = (all_labels[:, None] == classes[None, :]).astype(half)
    cond = time_columns(all_steps.astype(jnp.float32), columns, D) + jnp.dot(
        one_hot, class_table, preferred_element_type=jnp.float32
    )
    cond_half = silu_value(cond).astype(half)
    mod_part = jnp.dot(cond_half, w_ada, preferred_element_type=jnp.float32)
    modulation = lax.all_to_all(sum_ranks(mod_part, ranks), "dp", 0, 0, tiled=True)
    modulation = modulation.reshape(6, width)
    shift_a, scale_a, gate_a = (modulation[0], modulation[1], modulation[2])
    shift_m, scale_m, gate_m = (modulation[3], modulation[4], modulation[5])
    rows_in = latents_in[0].astype(jnp.float32)
    normed_a, inv_a = norm_rows(rows_in)
    mod_a = (normed_a * (1.0 + scale_a) + shift_a).astype(half)
    rest_a = fetch_rest(mod_a, ranks)
    grad_out = cotangent[0].astype(jnp.float32)
    grad_mlp = (grad_out * gate_m).astype(half)
    rest_grad_m = fetch_rest(grad_mlp, ranks)
    qkv_own = dot("td,dc->tc", mod_a, qkv_full).astype(half)
    qkv_rest = dot("td,dc->tc", rest_a, qkv_full).astype(half)
    projected = join(qkv_own, qkv_rest)
    tokens = projected.shape[0]
    queries = projected[:, :owned].reshape(tokens, heads_here, head_size)
    keys = projected[:, owned : 2 * owned].reshape(tokens, heads_here, head_size)
    values = projected[:, 2 * owned :].reshape(tokens, heads_here, head_size)
    mixed_rest, log_rest = attend(queries[mine:], keys, values, score_scale)
    mixed_rest_flat = mixed_rest.reshape(tokens - mine, owned)
    attn_away = return_rest(dot("tc,dc->td", mixed_rest_flat, proj_t), ranks)
    mixed_own, log_own = attend(queries[:mine], keys, values, score_scale)
    mixed_own_flat = mixed_own.reshape(mine, owned)
    attn_out = dot("tc,dc->td", mixed_own_flat, proj_t) + attn_away
    hidden = rows_in + gate_a * attn_out
    normed_m, inv_m = norm_rows(hidden)
    mod_m = (normed_m * (1.0 + scale_m) + shift_m).astype(half)
    rest_m = fetch_rest(mod_m, ranks)
    pre_own = dot("td,df->tf", mod_m, fc1_full)
    acts_own = gelu_value(pre_own).astype(half)
    pre_rest = dot("td,df->tf", rest_m, fc1_full)
    acts_rest = gelu_value(pre_rest).astype(half)
    mlp_away = return_rest(dot("tf,df->td", acts_rest, fc2_t), ranks)
    grad_pre_rest = (dot("td,df->tf", rest_grad_m, fc2_t) * gelu_slope(pre_rest)).astype(half)
    grad_mod_away = return_rest(dot("tf,df->td", grad_pre_rest, fc1_full), ranks)
    mlp_out = dot("tf,df->td", acts_own, fc2_t) + mlp_away
    block_out = (hidden + gate_m * mlp_out).astype(half)
    grad_gate_m = jnp.sum(grad_out * mlp_out, axis=0)
    grad_pre_own = (dot("td,df->tf", grad_mlp, fc2_t) * gelu_slope(pre_own)).astype(half)
    grad_mod_m = dot("tf,df->td", grad_pre_own, fc1_full) + grad_mod_away
    grad_fc2_t = dot("td,tf->df", join(grad_mlp, rest_grad_m), join(acts_own, acts_rest))
    grad_fc1 = dot("td,tf->df", join(mod_m, rest_m), join(grad_pre_own, grad_pre_rest))
    mlp_w_part = jnp.concatenate([grad_fc1.astype(half), grad_fc2_t.astype(half)], axis=1)
    mlp_w_part, grad_mod_m = lax.optimization_barrier((mlp_w_part, grad_mod_m))
    grad_mlp_w = lax.psum_scatter(mlp_w_part, "dp", scatter_dimension=0, tiled=True).astype(
        jnp.float32
    )
    grad_shift_m = jnp.sum(grad_mod_m, axis=0)
    grad_scale_m = jnp.sum(grad_mod_m * normed_m, axis=0)
    grad_hidden = grad_out + norm_back(grad_mod_m * (1.0 + scale_m), normed_m, inv_m)
    grad_gate_a = jnp.sum(grad_hidden * attn_out, axis=0)
    grad_attn = (grad_hidden * gate_a).astype(half)
    rest_grad_a = fetch_rest(grad_attn, ranks)
    grad_mixed_own = dot("td,dc->tc", grad_attn, proj_t).astype(half)
    grad_mixed_rest = dot("td,dc->tc", rest_grad_a, proj_t).astype(half)
    mixed_flat = join(mixed_own_flat, mixed_rest_flat)
    grad_proj_t = dot("td,tc->dc", join(grad_attn, rest_grad_a), mixed_flat)
    grad_mixed = join(grad_mixed_own, grad_mixed_rest)
    grads = attend_back(
        queries,
        keys,
        values,
        mixed_flat.reshape(tokens, heads_here, head_size),
        grad_mixed.reshape(tokens, heads_here, head_size),
        jnp.concatenate([log_own, log_rest], axis=1),
        score_scale,
    )
    grad_qkv = jnp.concatenate([g.astype(half).reshape(tokens, owned) for g in grads], axis=1)
    grad_a_away = return_rest(dot("tc,dc->td", grad_qkv[mine:], qkv_full), ranks)
    grad_w_qkv = dot("td,tc->dc", join(mod_a, rest_a), grad_qkv)
    attn_w_part = jnp.concatenate([grad_w_qkv.astype(half), grad_proj_t.astype(half)], axis=1)
    attn_w_part, grad_mlp_w = lax.optimization_barrier((attn_w_part, grad_mlp_w))
    grad_attn_w = lax.psum_scatter(attn_w_part, "dp", scatter_dimension=0, tiled=True).astype(
        jnp.float32
    )
    grad_mod_a = dot("tc,dc->td", grad_qkv[:mine], qkv_full) + grad_a_away
    grad_shift_a = jnp.sum(grad_mod_a, axis=0)
    grad_scale_a = jnp.sum(grad_mod_a * normed_a, axis=0)
    grad_input = grad_hidden + norm_back(grad_mod_a * (1.0 + scale_a), normed_a, inv_a)
    grad_mod_part = jnp.stack(
        [grad_shift_a, grad_scale_a, grad_gate_a, grad_shift_m, grad_scale_m, grad_gate_m]
    ).reshape(all_steps.shape[0], w_ada.shape[1])
    grad_modulation = lax.all_to_all(sum_ranks(grad_mod_part, ranks), "dp", 0, 0, tiled=True)
    grad_ada = jnp.einsum(
        "lc,lm->cm", cond_half.astype(jnp.float32), grad_modulation, precision=highest
    )
    grad_cond = lax.psum(
        jnp.einsum("lm,cm->lc", grad_modulation, w_ada.astype(jnp.float32), precision=highest), "dp"
    ) * silu_slope(cond)
    grad_table = jnp.einsum("ln,lc->nc", one_hot.astype(jnp.float32), grad_cond, precision=highest)
    return (
        block_out[None],
        grad_input[None],
        grad_table,
        grad_ada,
        jnp.stack([grad_attn_w[:, j * owned : (j + 1) * owned] for j in range(3)]),
        grad_attn_w[:, 3 * owned :].T,
        grad_mlp_w[:, : w_fc1.shape[1]],
        grad_mlp_w[:, w_fc1.shape[1] :].T,
    )


def solution(mesh):
    return jax.shard_map(
        functools.partial(shards, mesh.shape["tensor"]),
        mesh=mesh,
        in_specs=(
            P("dp", "tensor", None),
            P("dp"),
            P("dp"),
            P(None, "tensor"),
            P("tensor", "dp"),
            P(None, "dp", "tensor"),
            P("tensor", "dp"),
            P("dp", "tensor"),
            P("tensor", "dp"),
            P("dp", "tensor", None),
        ),
        out_specs=(
            P("dp", "tensor", None),
            P("dp", "tensor", None),
            P(None, "tensor"),
            P("tensor", "dp"),
            P(None, "dp", "tensor"),
            P("tensor", "dp"),
            P("dp", "tensor"),
            P("tensor", "dp"),
        ),
        check_vma=False,
    )
```

profile of v0, /device:TPU:0, one launch (start us, length us, event | category | flops | bytes accessed | tf_op | source)
XLA Modules:
  0.0 526.4 jit_solution(4783316110772384095)
XLA Ops:
  8.4 1.9 concatenate.48
  10.4 2.0 pad_maximum_fusion.6
  13.7 23.3 %all-gather = s32[16,1,2]{2,1,0:T(1,128)S(1)} all-gather(s32[1,1,2]{2,1,0:T(1,128)S(1)} %add_bitcast_fusion.1), channel_id=1, replica_groups=mesh['dp'=16,'tensor'=2] {'dp'}, dimensions={0}, use_global_device_ids=true | all-gather | bytes 136 | tf_op jit(solution)/shard_map/all_gather | solution.py:133
  38.2 1.5 collective-permute-start
  40.4 1.7 collective-permute-done
  42.8 3.5 all-to-all-start
  46.3 7.2 %all-to-all-done = f32[16,1,432]{2,1,0:T(1,128)S(1)} async-done(((f32[16,1,432]{2,1,0:T(1,128)}), f32[16,1,432]{2,1,0:T(1,128)S(1)}, u32[]{:S(2)}, u32[]{:S(2)}) %all-to-all-start) | async-done | bytes 27680 | tf_op jit(solution)/shard_map/all_to_all | solution.py:149
  55.0 1.5 collective-permute-start.1
  56.5 25.9 %collective-permute-done.1 = bf16[512,1152]{1,0:T(8,128)(2,1)S(1)} collective-permute-done((bf16[512,1152]{1,0:T(8,128)(2,1)S(1)}, bf16[512,1152]{1,0:T(8,128)(2,1)S(1)}, u32[]{:S(2)}, u32[]{:S(2)}) %collective-permute-start.1) | collective-permute-done | bytes 1179680 | tf_op jit(solution)/shard_map/ppermute | solution.py:88
  82.3 5.1 convolution_convert_fusion.6
  87.6 2.5 convolution_convert_fusion.7
  90.1 3.3 pad_maximum_fusion.3
  93.4 2.5 multiply_reduce_fusion
  95.9 3.5 exponential_reduce_fusion
  99.5 3.7 fusion.88
  103.2 3.2 convolution_convert_fusion.5
  106.4 1.6 collective-permute-start.2
  108.0 2.5 multiply_reduce_fusion.1
  110.5 3.5 exponential_reduce_fusion.1
  114.1 4.1 fusion.89
  118.2 14.8 %collective-permute-done.2 = bf16[512,1152]{1,0:T(8,128)(2,1)S(1)} collective-permute-done((bf16[512,1152]{1,0:T(8,128)(2,1)S(1)}, bf16[512,1152]{1,0:T(8,128)(2,1)S(1)}, u32[]{:S(2)}, u32[]{:S(2)}) %collective-permute-start.2) | collective-permute-done | bytes 1179680 | tf_op jit(solution)/shard_map/ppermute | solution.py:88
  133.0 4.9 fusion.132
  139.1 1.6 collective-permute-start.3
  142.5 25.7 %collective-permute-done.3 = bf16[512,1152]{1,0:T(8,128)(2,1)} collective-permute-done((bf16[512,1152]{1,0:T(8,128)(2,1)S(1)}, bf16[512,1152]{1,0:T(8,128)(2,1)}, u32[]{:S(2)}, u32[]{:S(2)}) %collective-permute-start.3) | collective-permute-done | bytes 1179680 | tf_op jit(solution)/shard_map/ppermute | solution.py:88
  168.1 8.4 %multiply_convert_fusion.1 = (bf16[512,2304]{1,0:T(8,128)(2,1)}, f32[512,2304]{1,0:T(8,128)S(1)}) fusion(bf16[512,1152]{1,0:T(8,128)(2,1)} %collective-permute-done.3, bf16[1152,4608]{1,0:T(8,128)(2,1)} %all-gather.6.cloned.1.call-done), kind=kOutput, calls=%fused_computation.39 | convolution fusion | flops 2728525824 | bytes 13565952 | tf_op jit(solution)/shard_map/td,df->tf/dot_general | solution.py:114
  176.5 13.8 %collective-permute-done.5 = bf16[512,1152]{1,0:T(8,128)(2,1)} collective-permute-done((bf16[512,1152]{1,0:T(8,128)(2,1)}, bf16[512,1152]{1,0:T(8,128)(2,1)}, u32[]{:S(2)}, u32[]{:S(2)}) %collective-permute-start.5) | collective-permute-done | bytes 1179680 | tf_op jit(solution)/shard_map/ppermute | solution.py:88
  190.4 6.6 %fusion.22 = bf16[512,2304]{1,0:T(8,128)(2,1)S(1)} fusion(f32[512,2304]{1,0:T(8,128)S(1)} %get-tuple-element.76, bf16[512,1152]{1,0:T(8,128)(2,1)} %collective-permute-done.5, bf16[1152,4608]{1,0:T(8,128)(2,1)S(1)} %copy-done.56), kind=kOutput, calls=%fused_computation.42 | convolution fusion | flops 2740322304 | bytes 13565952 | tf_op jit(solution)/shard_map/td,df->tf/dot_general | solution.py:114
  197.0 4.2 fusion.37
  201.2 1.5 collective-permute-start.6
  202.7 3.8 multiply_convert_fusion.2
  206.6 7.4 %fusion.21 = bf16[512,2304]{1,0:T(8,128)(2,1)S(1)} fusion(f32[512,2304]{1,0:T(8,128)S(1)} %get-tuple-element.74, bf16[512,1152]{1,0:T(8,128)(2,1)} %fusion.65, bf16[1152,4608]{1,0:T(8,128)(2,1)S(1)} %copy-done.56), kind=kOutput, calls=%fused_computation.41 | convolution fusion | flops 2740322304 | bytes 13565952 | tf_op jit(solution)/shard_map/td,df->tf/dot_general | solution.py:114
  214.0 9.1 %convolution_convert_fusion.1 = bf16[1152,2304]{1,0:T(8,128)(2,1)S(1)} fusion(bf16[512,2304]{1,0:T(8,128)(2,1)} %copy-done.62, bf16[512,2304]{1,0:T(8,128)(2,1)S(1)} %fusion.21, bf16[512,1152]{1,0:T(8,128)(2,1)} %collective-permute-done.3, bf16[512,1152]{1,0:T(8,128)(2,1)S(1)} %copy-done.28), kind=kOutput, calls=%fused_computation.11 | convolution fusion | flops 5452627968 | bytes 12386304 | tf_op jit(solution)/shard_map/td,tf->df/dot_general | solution.py:114
  223.2 7.9 %convolution_convert_fusion = bf16[1152,2304]{1,0:T(8,128)(2,1)S(1)} fusion(bf16[512,2304]{1,0:T(8,128)(2,1)S(1)} %copy-done.61, bf16[512,2304]{1,0:T(8,128)(2,1)S(1)} %get-tuple-element.73, bf16[512,1152]{1,0:T(8,128)(2,1)} %collective-permute-done.5, bf16[512,1152]{1,0:T(8,128)(2,1)} %fusion.65), kind=kOutput, calls=%fused_computation.10 | convolution fusion | flops 5452627968 | bytes 12386304 | tf_op jit(solution)/shard_map/td,tf->df/dot_general | solution.py:114
  231.1 4.5 pad_maximum_fusion
  235.6 8.2 %convert_add_fusion.2 = f32[512,1152]{1,0:T(8,128)} fusion(bf16[512,1152]{1,0:T(8,128)(2,1)} %collective-permute-done.6, bf16[512,2304]{1,0:T(8,128)(2,1)} %copy-done.58, bf16[1152,4608]{1,0:T(8,128)(2,1)} %all-gather.6.cloned.1.call-done), kind=kOutput, calls=%fused_computation.116 | convolution fusion | flops 2719088640 | bytes 11206656 | tf_op jit(solution)/shard_map/tf,df->td/dot_general | solution.py:114
  244.6 6.6 %fusion.40 = bf16[512,1152]{1,0:T(8,128)(2,1)S(1)} fusion(bf16[512,2304]{1,0:T(8,128)(2,1)} %get-tuple-element.75, bf16[1152,4608]{1,0:T(8,128)(2,1)} %all-gather.6.cloned.1.call-done), kind=kOutput, calls=%fused_computation.67 | convolution fusion | flops 2718498816 | bytes 8847360 | tf_op jit(solution)/shard_map/tf,df->td/dot_general | solution.py:114
  251.9 6.8 %fusion.27 = f32[512,1152]{1,0:T(8,128)S(1)} fusion(bf16[512,2304]{1,0:T(8,128)(2,1)S(1)} %copy-done.60, bf16[1152,4608]{1,0:T(8,128)(2,1)} %all-gather.6.cloned.1.call-done), kind=kOutput, calls=%fused_computation.55 | convolution fusion | flops 2717908992 | bytes 10027008 | tf_op jit(solution)/shard_map/tf,df->td/dot_general | solution.py:114
  258.7 1.6 multiply_reduce_fusion.2
  260.3 15.6 %collective-permute-done.4 = bf16[512,1152]{1,0:T(8,128)(2,1)S(1)} collective-permute-done((bf16[512,1152]{1,0:T(8,128)(2,1)S(1)}, bf16[512,1152]{1,0:T(8,128)(2,1)S(1)}, u32[]{:S(2)}, u32[]{:S(2)}) %collective-permute-start.4) | collective-permute-done | bytes 1179680 | tf_op jit(solution)/shard_map/ppermute | solution.py:88
  275.9 4.1 fusion.66
  282.2 13.3 %fusion.134 = f32[8,1024,1024]{2,1,0:T(8,128)} fusion(bf16[1024,8,72]{0,2,1:T(8,128)(2,1)S(1)} %bitcast.145, bf16[1024,8,72]{0,2,1:T(8,128)(2,1)S(1)} %bitcast.140), kind=kOutput, calls=%fused_computation.218 | convolution fusion | flops 1207959552 | bytes 35913728 | tf_op jit(solution)/shard_map/qhd,khd->hqk/dot_general | solution.py:71
  295.5 1.6 convolution_convert_fusion.11
  297.1 8.3 %collective-permute-done.7 = bf16[512,1152]{1,0:T(8,128)(2,1)S(1)} collective-permute-done((bf16[512,1152]{1,0:T(8,128)(2,1)S(1)}, bf16[512,1152]{1,0:T(8,128)(2,1)S(1)}, u32[]{:S(2)}, u32[]{:S(2)}) %collective-permute-start.7) | collective-permute-done | bytes 1179680 | tf_op jit(solution)/shard_map/ppermute | solution.py:88
  305.4 1.6 convolution_convert_fusion.10
  307.5 2.8 convolution_convert_fusion.3
  310.3 19.7 %multiply_convert_fusion = bf16[8,1024,1024]{2,1,0:T(8,128)(2,1)} fusion(f32[8,1024,1024]{2,1,0:T(8,128)} %fusion.134, f32[8,1024]{1,0:T(8,128)S(1)} %bitcast.170, f32[8,1024]{1,0:T(8,128)S(1)} %pad_maximum_fusion.7, bf16[1024,8,72]{0,2,1:T(8,128)(2,1)S(1)} %bitcast.143, bf16[1024,8,72]{0,2,1:T(8,128)(2,1)S(1)} %bitcast.149), kind=kOutput, calls=%fused_computation | convolution fusion | flops 1258291200 | bytes 52756480 | tf_op jit(solution)/shard_map/qhd,khd->hqk/dot_general | solution.py:77
  330.0 9.1 %convolution_convert_fusion.8 = bf16[8,72,1024]{2,1,0:T(8,128)(2,1)S(1)} fusion(bf16[1024,8,72]{0,2,1:T(8,128)(2,1)S(1)} %bitcast.146, bf16[8,1024,1024]{2,1,0:T(8,128)(2,1)} %multiply_convert_fusion), kind=kOutput, calls=%fused_computation.128 | convolution fusion | flops 1208549376 | bytes 19136512 | tf_op jit(solution)/shard_map/hqk,qhd->khd/dot_general | solution.py:83
  339.1 12.1 %convolution_convert_fusion.9 = bf16[8,72,1024]{2,1,0:T(8,128)(2,1)} fusion(bf16[1024,8,72]{0,2,1:T(8,128)(2,1)S(1)} %bitcast.141, bf16[8,1024,1024]{2,1,0:T(8,128)(2,1)} %multiply_convert_fusion), kind=kOutput, calls=%fused_computation.129 | convolution fusion | flops 1208549376 | bytes 19136512 | tf_op jit(solution)/shard_map/hqk,khd->qhd/dot_general | solution.py:82
  351.2 13.2 %fusion.85 = bf16[8,72,1024]{2,1,0:T(8,128)(2,1)S(1)} fusion(bf16[1024,8,72]{0,2,1:T(8,128)(2,1)S(1)} %bitcast.144, f32[8,1024,1024]{2,1,0:T(8,128)} %fusion.134, f32[8,1024]{1,0:T(8,128)} %copy-done.29), kind=kOutput, calls=%fused_computation.127 | convolution fusion | flops 1233715200 | bytes 35946496 | tf_op jit(solution)/shard_map/hqk,qhd->khd/dot_general | solution.py:74
  364.4 9.1 %convolution_convert_fusion.2 = bf16[1152,1728]{0,1:T(8,128)(2,1)S(1)} fusion(bf16[512,1152]{1,0:T(8,128)(2,1)} %copy-done.57, bf16[512,1152]{1,0:T(8,128)(2,1)} %copy-done.26, bf16[1024,576]{0,1:T(8,128)(2,1)S(1)} %bitcast.150, bf16[1024,576]{0,1:T(8,128)(2,1)S(1)} %bitcast.155, bf16[1024,576]{0,1:T(8,128)(2,1)S(1)} %bitcast.157), kind=kOutput, calls=%fused_computation.15 | convolution fusion | flops 4094189568 | bytes 9879552 | tf_op jit(solution)/shard_map/td,tc->dc/dot_general | solution.py:114
  373.6 2.8 pad_maximum_fusion.1
  376.4 2.2 convert_element_type.207
  378.6 8.6 %copy.25 = bf16[1152,2304]{1,0:T(8,128)(2,1)} copy(bf16[1152,2304]{0,1:T(8,128)(2,1)} %pad_maximum_fusion.1) | data formatting | bytes 10616832
  389.2 5.2 convolution_convert_fusion.4
  398.0 19.8 %collective-permute-done.8 = bf16[512,1152]{1,0:T(8,128)(2,1)S(1)} collective-permute-done((bf16[512,1152]{1,0:T(8,128)(2,1)S(1)}, bf16[512,1152]{1,0:T(8,128)(2,1)S(1)}, u32[]{:S(2)}, u32[]{:S(2)}) %collective-permute-start.8) | collective-permute-done | bytes 1179680 | tf_op jit(solution)/shard_map/ppermute | solution.py:88
  417.8 5.3 %fusion.63 = (f32[1152]{0:T(1024)S(1)}, f32[512]{0:T(512)}, f32[512]{0:T(512)}, f32[1152]{0:T(1024)S(1)}, f32[512,1152]{1,0:T(8,128)}) fusion(bf16[1,512,1152]{2,1,0:T(8,128)(2,1)S(1)} %copy-done.4, f32[512]{0:T(512)S(1)} %copy-done.53, f32[512]{0:T(512)S(1)} %copy-done.50, f32[1152]{0:T(1024)S(1)} %copy-done.38, ...), kind=kOutput, calls=%fused_computation.94 | convolution fusion | flops 2045506304 | bytes 10642432 | tf_op jit(solution)/shard_map/tc,dc->td/dot_general | solution.py:114
  424.3 1.4 stack.51
  425.7 1.5 reshape.147
  432.7 8.6 %all-to-all-start.1 = ((f32[16,1,432]{2,1,0:T(1,128)}), f32[16,1,432]{2,1,0:T(1,128)}, u32[]{:S(2)}, u32[]{:S(2)}) async-start(f32[16,1,432]{2,1,0:T(1,128)} %all_to_all.16), calls=%async_computation.1 | async-start | bytes 65536 | tf_op jit(solution)/shard_map/all_to_all | solution.py:231
  441.3 3.9 fusion.62
  445.2 2.8 all-to-all-done.1
  449.4 59.8 %psum.7 = f32[16,576]{1,0:T(8,128)S(1)} all-reduce(f32[16,576]{1,0:T(8,128)S(1)} %fusion.110), channel_id=1, replica_groups=mesh['dp'=16,'tensor'=2] {'dp'}, use_global_device_ids=true, to_apply=%region_19.20 | all-reduce | flops 9216 | bytes 73728 | tf_op jit(solution)/shard_map/psum | solution.py:235
  509.3 2.4 fusion.108
  511.7 3.3 fusion.101
  (207 shorter events, 30.9 us)
Async XLA Ops:
  7.2 29.9 %copy-start = (bf16[1000,576]{0,1:T(8,128)(2,1)S(1)}, bf16[1000,576]{0,1:T(8,128)(2,1)}, u32[]{:S(2)}) copy-start(bf16[1000,576]{0,1:T(8,128)(2,1)} %param.13) | copy-start | bytes 3456004
  7.2 30.4 %copy-start.24 = (bf16[576,432]{0,1:T(8,128)(2,1)S(1)}, bf16[576,432]{0,1:T(8,128)(2,1)}, u32[]{:S(2)}) copy-start(bf16[576,432]{0,1:T(8,128)(2,1)} %param.14) | copy-start | bytes 1492996
  7.2 75.1 %all-gather.4.cloned.1.call-start = ((), (), s32[]{:S(2)}) async-start(), calls=%async_computation.4 | async-start | bytes 5640192 | tf_op jit(solution)/shard_map/all_gather | solution.py:135
  8.4 31.3 %copy-start.2 = (bf16[1,512,1152]{2,1,0:T(8,128)(2,1)S(1)}, bf16[1,512,1152]{2,1,0:T(8,128)(2,1)}, u32[]{:S(2)}) copy-start(bf16[1,512,1152]{2,1,0:T(8,128)(2,1)} %param.10) | copy-start | bytes 3538948
  10.3 157.8 %all-gather.6.cloned.1.call-start = ((), (), s32[]{:S(2)}) async-start(), calls=%async_computation.5 | async-start | bytes 11280384 | tf_op jit(solution)/shard_map/all_gather | solution.py:138
  38.2 3.9 collective-permute-start
  39.9 47.6 %copy-start.49 = (f32[512]{0:T(512)}, f32[512]{0:T(512)S(1)}, u32[]{:S(2)}) copy-start(f32[512]{0:T(512)S(1)} %broadcast_multiply_fusion.5) | copy-start | bytes 6148
  42.8 10.7 %all-to-all-start = ((f32[16,1,432]{2,1,0:T(1,128)}), f32[16,1,432]{2,1,0:T(1,128)S(1)}, u32[]{:S(2)}, u32[]{:S(2)}) async-start(f32[16,1,432]{2,1,0:T(1,128)} %copy.22), calls=%async_computation | async-start | bytes 65536 | tf_op jit(solution)/shard_map/all_to_all | solution.py:149
  46.3 330.1 %reduce-scatter.5.cloned.1.call-start = ((), (), s32[]{:S(2)}) async-start(), calls=%async_computation.6 | async-start | bytes 11280384 | tf_op jit(solution)/shard_map/reduce_scatter | solution.py:193
  46.3 41.2 %copy-start.52 = (f32[512]{0:T(512)}, f32[512]{0:T(512)S(1)}, u32[]{:S(2)}) copy-start(f32[512]{0:T(512)S(1)} %add_rsqrt_fusion.1) | copy-start | bytes 6148
  54.9 32.6 %copy-start.26 = (bf16[512,1152]{1,0:T(8,128)(2,1)}, bf16[512,1152]{1,0:T(8,128)(2,1)S(1)}, u32[]{:S(2)}) copy-start(bf16[512,1152]{1,0:T(8,128)(2,1)S(1)} %fusion.57) | copy-start | bytes 3538948
  55.0 27.4 %collective-permute-start.1 = (bf16[512,1152]{1,0:T(8,128)(2,1)S(1)}, bf16[512,1152]{1,0:T(8,128)(2,1)S(1)}, u32[]{:S(2)}, u32[]{:S(2)}) collective-permute-start(bf16[512,1152]{1,0:T(8,128)(2,1)S(1)} %fusion.57), channel_id=1, source_target_pairs={{0,1},{1,0},{2,3},{3,2},{4,5},{5,4},{6,7},{7,6},{8,9},{9,8},{10,11... | collective-permute-start | bytes 3538952 | tf_op jit(solution)/shard_map/ppermute | solution.py:88
  82.3 5.2 copy-start.57
  82.3 5.2 copy-start.31
  93.4 20.6 %copy-start.8 = (bf16[1024,576]{0,1:T(8,128)(2,1)}, bf16[1024,576]{0,1:T(8,128)(2,1)S(1)}, u32[]{:S(2)}) copy-start(bf16[1024,576]{0,1:T(8,128)(2,1)S(1)} %get-tuple-element.55) | copy-start | bytes 3538948
  103.2 7.3 %copy-start.22 = (bf16[8,72,512]{2,1,0:T(8,128)(2,1)}, bf16[8,72,512]{2,1,0:T(8,128)(2,1)S(1)}, u32[]{:S(2)}) copy-start(bf16[8,72,512]{2,1,0:T(8,128)(2,1)S(1)} %fusion.88) | copy-start | bytes 1769476
  106.4 26.6 %collective-permute-start.2 = (bf16[512,1152]{1,0:T(8,128)(2,1)S(1)}, bf16[512,1152]{1,0:T(8,128)(2,1)S(1)}, u32[]{:S(2)}, u32[]{:S(2)}) collective-permute-start(bf16[512,1152]{1,0:T(8,128)(2,1)S(1)} %convolution_convert_fusion.5), channel_id=1, source_target_pairs={{0,1},{1,0},{2,3},{3,2},{4,5},{5,4},{6,7},{7,6},{8,9},{9,8},{10,11... | collective-permute-start | bytes 3538952 | tf_op jit(solution)/shard_map/ppermute | solution.py:88
  114.1 18.9 %copy-start.3 = (bf16[1,512,1152]{2,1,0:T(8,128)(2,1)S(1)}, bf16[1,512,1152]{2,1,0:T(8,128)(2,1)}, u32[]{:S(2)}) copy-start(bf16[1,512,1152]{2,1,0:T(8,128)(2,1)} %param.10) | copy-start | bytes 3538948
  114.1 18.9 %copy-start.39 = (f32[1152]{0:T(1024)S(1)}, f32[1152]{0:T(1024)}, u32[]{:S(2)}) copy-start(f32[1152]{0:T(1024)} %get-tuple-element.45) | copy-start | bytes 13828
  118.2 19.7 %copy-start.13 = (bf16[8,72,512]{2,1,0:T(8,128)(2,1)}, bf16[8,72,512]{2,1,0:T(8,128)(2,1)S(1)}, u32[]{:S(2)}) copy-start(bf16[8,72,512]{2,1,0:T(8,128)(2,1)S(1)} %fusion.89) | copy-start | bytes 1769476
  139.1 29.0 %collective-permute-start.3 = (bf16[512,1152]{1,0:T(8,128)(2,1)S(1)}, bf16[512,1152]{1,0:T(8,128)(2,1)}, u32[]{:S(2)}, u32[]{:S(2)}) collective-permute-start(bf16[512,1152]{1,0:T(8,128)(2,1)S(1)} %add_convert_fusion.1), channel_id=1, source_target_pairs={{0,1},{1,0},{2,3},{3,2},{4,5},{5,4},{6,7},{7,6},{8,9},{9,8},{10,11... | collective-permute-start | bytes 3538952 | tf_op jit(solution)/shard_map/ppermute | solution.py:88
  141.9 48.4 %collective-permute-start.5 = (bf16[512,1152]{1,0:T(8,128)(2,1)}, bf16[512,1152]{1,0:T(8,128)(2,1)}, u32[]{:S(2)}, u32[]{:S(2)}) collective-permute-start(bf16[512,1152]{1,0:T(8,128)(2,1)} %fusion.65), channel_id=1, source_target_pairs={{0,1},{1,0},{2,3},{3,2},{4,5},{5,4},{6,7},{7,6},{8,9},{9,8},{10,11... | collective-permute-start | bytes 3538952 | tf_op jit(solution)/shard_map/ppermute | solution.py:88
  168.1 22.2 %copy-start.56 = (bf16[1152,4608]{1,0:T(8,128)(2,1)S(1)}, bf16[1152,4608]{1,0:T(8,128)(2,1)}, u32[]{:S(2)}) copy-start(bf16[1152,4608]{1,0:T(8,128)(2,1)} %all-gather.6.cloned.1.call-done) | copy-start | bytes 31850500
  197.0 5.7 %copy-start.28 = (bf16[512,1152]{1,0:T(8,128)(2,1)S(1)}, bf16[512,1152]{1,0:T(8,128)(2,1)}, u32[]{:S(2)}) copy-start(bf16[512,1152]{1,0:T(8,128)(2,1)} %copy-done.27) | copy-start | bytes 3538948
  201.2 34.4 %collective-permute-start.6 = (bf16[512,1152]{1,0:T(8,128)(2,1)}, bf16[512,1152]{1,0:T(8,128)(2,1)}, u32[]{:S(2)}, u32[]{:S(2)}) collective-permute-start(bf16[512,1152]{1,0:T(8,128)(2,1)} %fusion.37), channel_id=1, source_target_pairs={{0,1},{1,0},{2,3},{3,2},{4,5},{5,4},{6,7},{7,6},{8,9},{9,8},{10,11... | collective-permute-start | bytes 3538952 | tf_op jit(solution)/shard_map/ppermute | solution.py:88
  206.5 16.6 %copy-start.59 = (bf16[512,2304]{1,0:T(8,128)(2,1)}, bf16[512,2304]{1,0:T(8,128)(2,1)S(1)}, u32[]{:S(2)}) copy-start(bf16[512,2304]{1,0:T(8,128)(2,1)S(1)} %get-tuple-element.73) | copy-start | bytes 7077892
  214.0 9.2 %copy-start.58 = (bf16[512,2304]{1,0:T(8,128)(2,1)}, bf16[512,2304]{1,0:T(8,128)(2,1)S(1)}, u32[]{:S(2)}) copy-start(bf16[512,2304]{1,0:T(8,128)(2,1)S(1)} %fusion.21) | copy-start | bytes 7077892
  214.0 9.2 %copy-start.61 = (bf16[512,2304]{1,0:T(8,128)(2,1)S(1)}, bf16[512,2304]{1,0:T(8,128)(2,1)}, u32[]{:S(2)}) copy-start(bf16[512,2304]{1,0:T(8,128)(2,1)} %get-tuple-element.75) | copy-start | bytes 7077892
  243.8 272.4 %reduce-scatter.7.cloned.1.call-start = ((), (), s32[]{:S(2)}) async-start(), calls=%async_computation.7 | async-start | bytes 5640192
  244.6 65.7 %copy-start.29 = (f32[8,1024]{1,0:T(8,128)}, f32[8,1024]{1,0:T(8,128)S(1)}, u32[]{:S(2)}) copy-start(f32[8,1024]{1,0:T(8,128)S(1)} %pad_maximum_fusion.7) | copy-start | bytes 98308
  244.6 7.3 %copy-start.60 = (bf16[512,2304]{1,0:T(8,128)(2,1)S(1)}, bf16[512,2304]{1,0:T(8,128)(2,1)}, u32[]{:S(2)}) copy-start(bf16[512,2304]{1,0:T(8,128)(2,1)} %copy-done.59) | copy-start | bytes 7077892
  251.2 7.4 %copy-start.10 = (f32[512,1152]{1,0:T(8,128)S(1)}, f32[512,1152]{1,0:T(8,128)}, u32[]{:S(2)}) copy-start(f32[512,1152]{1,0:T(8,128)} %convert_add_fusion.2) | copy-start | bytes 7077892
  251.2 7.4 %copy-start.34 = (f32[1152]{0:T(1024)S(1)}, f32[1152]{0:T(1024)}, u32[]{:S(2)}) copy-start(f32[1152]{0:T(1024)} %get-tuple-element.42) | copy-start | bytes 13828
  251.2 7.4 %copy-start.42 = (f32[512]{0:T(512)S(1)}, f32[512]{0:T(512)}, u32[]{:S(2)}) copy-start(f32[512]{0:T(512)} %copy-done.41) | copy-start | bytes 6148
  251.2 7.4 %copy-start.45 = (f32[512]{0:T(512)S(1)}, f32[512]{0:T(512)}, u32[]{:S(2)}) copy-start(f32[512]{0:T(512)} %copy-done.44) | copy-start | bytes 6148
  251.2 24.7 %collective-permute-start.4 = (bf16[512,1152]{1,0:T(8,128)(2,1)S(1)}, bf16[512,1152]{1,0:T(8,128)(2,1)S(1)}, u32[]{:S(2)}, u32[]{:S(2)}) collective-permute-start(bf16[512,1152]{1,0:T(8,128)(2,1)S(1)} %fusion.40), channel_id=1, source_target_pairs={{0,1},{1,0},{2,3},{3,2},{4,5},{5,4},{6,7},{7,6},{8,9},{9,8},{10,11... | collective-permute-start | bytes 3538952 | tf_op jit(solution)/shard_map/ppermute | solution.py:88
  258.7 17.2 %copy-start.11 = (f32[512,1152]{1,0:T(8,128)S(1)}, f32[512,1152]{1,0:T(8,128)}, u32[]{:S(2)}) copy-start(f32[512,1152]{1,0:T(8,128)} %get-tuple-element.72) | copy-start | bytes 7077892
  258.7 17.2 %copy-start.16 = (bf16[512,1152]{1,0:T(8,128)(2,1)S(1)}, bf16[512,1152]{1,0:T(8,128)(2,1)}, u32[]{:S(2)}) copy-start(bf16[512,1152]{1,0:T(8,128)(2,1)} %copy-done.15) | copy-start | bytes 3538948
  258.7 17.2 %copy-start.20 = (bf16[1,512,1152]{2,1,0:T(8,128)(2,1)S(1)}, bf16[1,512,1152]{2,1,0:T(8,128)(2,1)}, u32[]{:S(2)}) copy-start(bf16[1,512,1152]{2,1,0:T(8,128)(2,1)} %param.19) | copy-start | bytes 3538948
  258.7 17.2 %copy-start.36 = (f32[1152]{0:T(1024)S(1)}, f32[1152]{0:T(1024)}, u32[]{:S(2)}) copy-start(f32[1152]{0:T(1024)} %get-tuple-element.40) | copy-start | bytes 13828
  275.9 5.5 %copy-start.40 = (f32[1152]{0:T(1024)S(1)}, f32[1152]{0:T(1024)}, u32[]{:S(2)}) copy-start(f32[1152]{0:T(1024)} %get-tuple-element.45) | copy-start | bytes 13828
  275.9 19.6 %slice-start.1 = ((s8[5308416]{0:T(1024)(128)(4,1)}), s8[4194304]{0:T(1024)(128)(4,1)S(1)}, s32[]{:S(2)}) async-start(s8[5308416]{0:T(1024)(128)(4,1)} %bitcast.164), calls=%async_computation.9 | async-start | bytes 8388608
  281.6 23.8 %collective-permute-start.7 = (bf16[512,1152]{1,0:T(8,128)(2,1)S(1)}, bf16[512,1152]{1,0:T(8,128)(2,1)S(1)}, u32[]{:S(2)}, u32[]{:S(2)}) collective-permute-start(bf16[512,1152]{1,0:T(8,128)(2,1)S(1)} %multiply_convert_fusion.3), channel_id=1, source_target_pairs={{0,1},{1,0},{2,3},{3,2},{4,5},{5,4},{6,7},{7,6},{8,9},{9,8},{10,11... | collective-permute-start | bytes 3538952 | tf_op jit(solution)/shard_map/ppermute | solution.py:88
  282.2 13.3 %slice-start.2 = ((s8[5308416]{0:T(1024)(128)(4,1)}), s8[1114112]{0:T(1024)(128)(4,1)S(1)}, s32[]{:S(2)}) async-start(s8[5308416]{0:T(1024)(128)(4,1)} %bitcast.164), calls=%async_computation.10 | async-start | bytes 2228224
  297.1 10.0 %copy-start.14 = (bf16[8,72,512]{2,1,0:T(8,128)(2,1)S(1)}, bf16[8,72,512]{2,1,0:T(8,128)(2,1)}, u32[]{:S(2)}) copy-start(bf16[8,72,512]{2,1,0:T(8,128)(2,1)} %copy-done.13) | copy-start | bytes 1769476
  297.1 10.0 %copy-start.23 = (bf16[8,72,512]{2,1,0:T(8,128)(2,1)S(1)}, bf16[8,72,512]{2,1,0:T(8,128)(2,1)}, u32[]{:S(2)}) copy-start(bf16[8,72,512]{2,1,0:T(8,128)(2,1)} %copy-done.22) | copy-start | bytes 1769476
  351.2 13.2 %copy-start.17 = (bf16[8,72,1024]{2,1,0:T(8,128)(2,1)S(1)}, bf16[8,72,1024]{2,1,0:T(8,128)(2,1)}, u32[]{:S(2)}) copy-start(bf16[8,72,1024]{2,1,0:T(8,128)(2,1)} %convolution_convert_fusion.9) | copy-start | bytes 3538948
  364.4 9.2 %copy-start.25 = (bf16[1152,576]{0,1:T(8,128)(2,1)S(1)}, bf16[1152,576]{0,1:T(8,128)(2,1)}, u32[]{:S(2)}) copy-start(bf16[1152,576]{0,1:T(8,128)(2,1)} %convolution_convert_fusion.3) | copy-start | bytes 3981316
  388.4 29.3 %slice-start.3 = ((s8[5308416]{0:T(1024)(128)(4,1)}), s8[4194304]{0:T(1024)(128)(4,1)S(1)}, s32[]{:S(2)}) async-start(s8[5308416]{0:T(1024)(128)(4,1)} %bitcast.166), calls=%async_computation.11 | async-start | bytes 8388608
  389.1 6.5 %copy-start.48 = (f32[1152]{0:T(1024)S(1)}, f32[1152]{0:T(1024)}, u32[]{:S(2)}) copy-start(f32[1152]{0:T(1024)} %get-tuple-element.32) | copy-start | bytes 13828
  389.1 7.1 %copy-start.43 = (f32[1152]{0:T(1024)S(1)}, f32[1152]{0:T(1024)}, u32[]{:S(2)}) copy-start(f32[1152]{0:T(1024)} %get-tuple-element.50) | copy-start | bytes 13828
  389.1 8.3 %copy-start.47 = (f32[1152]{0:T(1024)S(1)}, f32[1152]{0:T(1024)}, u32[]{:S(2)}) copy-start(f32[1152]{0:T(1024)} %get-tuple-element.38) | copy-start | bytes 13828
  389.1 28.6 %copy-start.4 = (bf16[1,512,1152]{2,1,0:T(8,128)(2,1)S(1)}, bf16[1,512,1152]{2,1,0:T(8,128)(2,1)}, u32[]{:S(2)}) copy-start(bf16[1,512,1152]{2,1,0:T(8,128)(2,1)} %param.10) | copy-start | bytes 3538948
  389.1 28.6 %slice-start.4 = ((s8[5308416]{0:T(1024)(128)(4,1)}), s8[1114112]{0:T(1024)(128)(4,1)S(1)}, s32[]{:S(2)}) async-start(s8[5308416]{0:T(1024)(128)(4,1)} %bitcast.166), calls=%async_computation.12 | async-start | bytes 2228224
  389.1 28.6 %copy-start.38 = (f32[1152]{0:T(1024)S(1)}, f32[1152]{0:T(1024)}, u32[]{:S(2)}) copy-start(f32[1152]{0:T(1024)} %copy-done.37) | copy-start | bytes 13828
  389.1 28.6 %copy-start.50 = (f32[512]{0:T(512)S(1)}, f32[512]{0:T(512)}, u32[]{:S(2)}) copy-start(f32[512]{0:T(512)} %copy-done.49) | copy-start | bytes 6148
  389.2 28.6 %copy-start.53 = (f32[512]{0:T(512)S(1)}, f32[512]{0:T(512)}, u32[]{:S(2)}) copy-start(f32[512]{0:T(512)} %copy-done.52) | copy-start | bytes 6148
  394.3 23.4 %collective-permute-start.8 = (bf16[512,1152]{1,0:T(8,128)(2,1)S(1)}, bf16[512,1152]{1,0:T(8,128)(2,1)S(1)}, u32[]{:S(2)}, u32[]{:S(2)}) collective-permute-start(bf16[512,1152]{1,0:T(8,128)(2,1)S(1)} %convolution_convert_fusion.4), channel_id=1, source_target_pairs={{0,1},{1,0},{2,3},{3,2},{4,5},{5,4},{6,7},{7,6},{8,9},{9,8},{10,11... | collective-permute-start | bytes 3538952 | tf_op jit(solution)/shard_map/ppermute | solution.py:88
  397.9 43.4 %copy-start.6 = (f32[512,1152]{1,0:T(8,128)S(1)}, f32[512,1152]{1,0:T(8,128)}, u32[]{:S(2)}) copy-start(f32[512,1152]{1,0:T(8,128)} %copy-done.5) | copy-start | bytes 7077892
  398.0 43.4 %copy-start.51 = (f32[512]{0:T(512)S(1)}, f32[512]{0:T(512)}, u32[]{:S(2)}) copy-start(f32[512]{0:T(512)} %copy-done.49) | copy-start | bytes 6148
  398.0 43.4 %copy-start.54 = (f32[512]{0:T(512)S(1)}, f32[512]{0:T(512)}, u32[]{:S(2)}) copy-start(f32[512]{0:T(512)} %copy-done.52) | copy-start | bytes 6148
  427.2 4.1 collective-permute-start.9
  432.7 15.3 %all-to-all-start.1 = ((f32[16,1,432]{2,1,0:T(1,128)}), f32[16,1,432]{2,1,0:T(1,128)}, u32[]{:S(2)}, u32[]{:S(2)}) async-start(f32[16,1,432]{2,1,0:T(1,128)} %all_to_all.16), calls=%async_computation.1 | async-start | bytes 65536 | tf_op jit(solution)/shard_map/all_to_all | solution.py:231
  445.2 69.8 %copy-start.12 = (f32[72,4608]{1,0:T(8,128)S(1)}, f32[72,4608]{1,0:T(8,128)}, u32[]{:S(2)}) copy-start(f32[72,4608]{1,0:T(8,128)} %convert_element_type.207) | copy-start | bytes 3981316
  (20 other events, 46.8 us)
Sparse Core Ops, SparseCore 0:
  10.7 59.4 all-gather.3
  73.0 86.9 all-gather.5
  243.9 120.1 reduce-scatter.4
  387.3 80.5 reduce-scatter.6
where the time goes:
time: 534 us; the launch traced here: 526 us
  matrix products  198 us (37%)
  waiting for transfers between devices  137 us (26%)
  blocking collectives  83.1 us (16%)
  other arithmetic  41.1 us (8%)
  local copies, waits for them, and re-layouts  27.7 us (5%)
  starting transfers between devices  23.1 us (4%)
  between operations  16.3 us (3%)
    ppermute x10, waiting for transfers between devices, from_rank(): lax.ppermute(value, 'tensor', [(i, (i - step) % ranks) for i in range(ran...  127 us
    dot_general x20, matrix products, dot(): return jnp.einsum(spec, left, right, preferred_element_type=jnp.float32)  110 us
    psum x1, blocking collectives, shards(): lax.psum(jnp.einsum('lm,cm->lc', grad_modulation, w_ada.astype(jnp.float3...  59.8 us
    all_gather x1, blocking collectives, shards(): lax.all_gather(jnp.stack([steps, labels], axis=1), 'dp', axis=0, tiled=True)  23.3 us
    dot_general x1, matrix products, attend_back(): jnp.einsum('qhd,khd->hqk', grad_mixed, values, preferred_element_type=jnp...  19.7 us
    unnamed x138, local copies, waits for them, and re-layouts  15.4 us
    dot_general x1, matrix products, attend_back(): jnp.einsum('qhd,khd->hqk', queries, keys, preferred_element_type=jnp.floa...  13.3 us
    dot_general x1, matrix products, attend_back(): jnp.einsum('hqk,qhd->khd', probs.astype(jnp.bfloat16), grad_mixed, prefer...  13.2 us
  transfers between devices with their start and end apart: 16, of which 11 were waited for; matrix products, arithmetic and copies ran while one was open for 43% of the time, Pallas kernels for 0%

commit v1 on v0

--- a/solution.py
+++ b/solution.py
@@ -232,8 +232,12 @@
     grad_ada = jnp.einsum(
         "lc,lm->cm", cond_half.astype(jnp.float32), grad_modulation, precision=highest
     )
-    grad_cond = lax.psum(
-        jnp.einsum("lm,cm->lc", grad_modulation, w_ada.astype(jnp.float32), precision=highest), "dp"
+    grad_cond = jnp.sum(
+        lax.all_gather(
+            jnp.einsum("lm,cm->lc", grad_modulation, w_ada.astype(jnp.float32), precision=highest),
+            "dp",
+        ),
+        axis=0,
     ) * silu_slope(cond)
     grad_table = jnp.einsum("ln,lc->nc", one_hot.astype(jnp.float32), grad_cond, precision=highest)
     return (

time: 534 us -> 497 us (0.931)
  blocking collectives: 83.1 us -> 46.6 us
    psum x1 -> x0, blocking collectives: 59.8 us -> none  [shards(): lax.psum(jnp.einsum('lm,cm->lc', grad_modulation, w_ada.astype(jnp.float3...]
    all_gather x0 -> x1, blocking collectives: none -> 23.3 us  [shards(): lax.all_gather(jnp.einsum('lm,cm->lc', grad_modulation, w_ada.astype(jnp....]
    unnamed x138 -> x142, local copies, waits for them, and re-layouts: 15.4 us -> 15.4 us
  transfers between devices with their start and end apart: 16 -> 16, of which waited for: 11 -> 11; matrix products, arithmetic and copies ran while one was open for 43% -> 46% of each run, Pallas kernels for 0% -> 0%
where the time goes in v1:
time: 497 us; the launch traced here: 489 us
  matrix products  198 us (40%)
  waiting for transfers between devices  137 us (28%)
  blocking collectives  46.6 us (9%)
  other arithmetic  41.1 us (8%)
  local copies, waits for them, and re-layouts  27.7 us (6%)
  starting transfers between devices  22.9 us (5%)
  between operations  16.3 us (3%)
    ppermute x10, waiting for transfers between devices, from_rank(): lax.ppermute(value, 'tensor', [(i, (i - step) % ranks) for i in range(ran...  127 us
    dot_general x20, matrix products, dot(): return jnp.einsum(spec, left, right, preferred_element_type=jnp.float32)  110 us
    all_gather x1, blocking collectives, shards(): lax.all_gather(jnp.einsum('lm,cm->lc', grad_modulation, w_ada.astype(jnp....  23.3 us
    all_gather x1, blocking collectives, shards(): lax.all_gather(jnp.stack([steps, labels], axis=1), 'dp', axis=0, tiled=True)  23.3 us
    dot_general x1, matrix products, attend_back(): jnp.einsum('qhd,khd->hqk', grad_mixed, values, preferred_element_type=jnp...  19.7 us
    unnamed x142, local copies, waits for them, and re-layouts  15.4 us
    dot_general x1, matrix products, attend_back(): jnp.einsum('qhd,khd->hqk', queries, keys, preferred_element_type=jnp.floa...  13.3 us
    dot_general x1, matrix products, attend_back(): jnp.einsum('hqk,qhd->khd', probs.astype(jnp.bfloat16), grad_mixed, prefer...  13.2 us
  transfers between devices with their start and end apart: 16, of which 11 were waited for; matrix products, arithmetic and copies ran while one was open for 46% of the time, Pallas kernels for 0%

profile of v1, /device:TPU:0, one launch (start us, length us, event | category | flops | bytes accessed | tf_op | source)
XLA Modules:
  0.0 489.2 jit_solution(12180305109341438883)
XLA Ops:
  8.4 1.9 concatenate.48
  10.4 2.0 pad_maximum_fusion.6
  13.7 23.3 %all-gather.1 = s32[16,1,2]{2,1,0:T(1,128)S(1)} all-gather(s32[1,1,2]{2,1,0:T(1,128)S(1)} %add_bitcast_fusion.1), channel_id=1, replica_groups=mesh['dp'=16,'tensor'=2] {'dp'}, dimensions={0}, use_global_device_ids=true | all-gather | bytes 136 | tf_op jit(solution)/shard_map/all_gather | solution.py:133
  38.2 1.5 collective-permute-start
  40.4 1.7 collective-permute-done
  42.8 3.5 all-to-all-start
  46.3 7.2 %all-to-all-done = f32[16,1,432]{2,1,0:T(1,128)S(1)} async-done(((f32[16,1,432]{2,1,0:T(1,128)}), f32[16,1,432]{2,1,0:T(1,128)S(1)}, u32[]{:S(2)}, u32[]{:S(2)}) %all-to-all-start) | async-done | bytes 27680 | tf_op jit(solution)/shard_map/all_to_all | solution.py:149
  55.0 1.5 collective-permute-start.1
  56.5 25.9 %collective-permute-done.1 = bf16[512,1152]{1,0:T(8,128)(2,1)S(1)} collective-permute-done((bf16[512,1152]{1,0:T(8,128)(2,1)S(1)}, bf16[512,1152]{1,0:T(8,128)(2,1)S(1)}, u32[]{:S(2)}, u32[]{:S(2)}) %collective-permute-start.1) | collective-permute-done | bytes 1179680 | tf_op jit(solution)/shard_map/ppermute | solution.py:88
  82.3 5.1 %convolution_convert_fusion.6 = bf16[512,1728]{0,1:T(8,128)(2,1)S(1)} fusion(bf16[512,1152]{1,0:T(8,128)(2,1)S(1)} %collective-permute-done.1, bf16[1152,2304]{1,0:T(8,128)(2,1)} %all-gather.5.cloned.1.call-done), kind=kOutput, calls=%fused_computation.70 | convolution fusion | flops 2039316480 | bytes 7077888 | tf_op jit(solution)/shard_map/td,dc->tc/dot_general | solution.py:114
  87.6 2.6 convolution_convert_fusion.7
  90.2 3.3 pad_maximum_fusion.3
  93.5 2.5 multiply_reduce_fusion
  96.0 3.5 exponential_reduce_fusion
  99.5 3.7 fusion.88
  103.3 3.2 convolution_convert_fusion.5
  106.4 1.6 collective-permute-start.2
  108.0 2.5 multiply_reduce_fusion.1
  110.5 3.5 exponential_reduce_fusion.1
  114.1 4.1 fusion.89
  118.3 14.8 %collective-permute-done.2 = bf16[512,1152]{1,0:T(8,128)(2,1)S(1)} collective-permute-done((bf16[512,1152]{1,0:T(8,128)(2,1)S(1)}, bf16[512,1152]{1,0:T(8,128)(2,1)S(1)}, u32[]{:S(2)}, u32[]{:S(2)}) %collective-permute-start.2) | collective-permute-done | bytes 1179680 | tf_op jit(solution)/shard_map/ppermute | solution.py:88
  133.0 4.9 %fusion.132 = (f32[512]{0:T(512)S(1)}, f32[512,1152]{1,0:T(8,128)S(1)}, f32[512,1152]{1,0:T(8,128)}) fusion(bf16[512,1152]{1,0:T(8,128)(2,1)S(1)} %collective-permute-done.2, f32[1152]{0:T(1024)S(1)} %copy-done.40, bf16[1,512,1152]{2,1,0:T(8,128)(2,1)S(1)} %copy-done.3, bf16[512,576]{0,1:T(8,128)(2,1)S(1)} %bitcast.153, ...), kind=kOutput, calls=%fused_computation.217 | convolution fusion | flops 683015680 | bytes 9148928 | tf_op jit(solution)/shard_map/tc,dc->td/dot_general | solution.py:114
  139.1 1.6 collective-permute-start.3
  142.5 25.7 %collective-permute-done.3 = bf16[512,1152]{1,0:T(8,128)(2,1)} collective-permute-done((bf16[512,1152]{1,0:T(8,128)(2,1)S(1)}, bf16[512,1152]{1,0:T(8,128)(2,1)}, u32[]{:S(2)}, u32[]{:S(2)}) %collective-permute-start.3) | collective-permute-done | bytes 1179680 | tf_op jit(solution)/shard_map/ppermute | solution.py:88
  168.2 8.4 %multiply_convert_fusion.1 = (bf16[512,2304]{1,0:T(8,128)(2,1)}, f32[512,2304]{1,0:T(8,128)S(1)}) fusion(bf16[512,1152]{1,0:T(8,128)(2,1)} %collective-permute-done.3, bf16[1152,4608]{1,0:T(8,128)(2,1)} %all-gather.7.cloned.1.call-done), kind=kOutput, calls=%fused_computation.39 | convolution fusion | flops 2728525824 | bytes 13565952 | tf_op jit(solution)/shard_map/td,df->tf/dot_general | solution.py:114
  176.5 13.8 %collective-permute-done.5 = bf16[512,1152]{1,0:T(8,128)(2,1)} collective-permute-done((bf16[512,1152]{1,0:T(8,128)(2,1)}, bf16[512,1152]{1,0:T(8,128)(2,1)}, u32[]{:S(2)}, u32[]{:S(2)}) %collective-permute-start.5) | collective-permute-done | bytes 1179680 | tf_op jit(solution)/shard_map/ppermute | solution.py:88
  190.3 6.6 %fusion.22 = bf16[512,2304]{1,0:T(8,128)(2,1)S(1)} fusion(f32[512,2304]{1,0:T(8,128)S(1)} %get-tuple-element.76, bf16[512,1152]{1,0:T(8,128)(2,1)} %collective-permute-done.5, bf16[1152,4608]{1,0:T(8,128)(2,1)S(1)} %copy-done.58), kind=kOutput, calls=%fused_computation.42 | convolution fusion | flops 2740322304 | bytes 13565952 | tf_op jit(solution)/shard_map/td,df->tf/dot_general | solution.py:114
  197.0 4.2 fusion.37
  201.2 1.5 collective-permute-start.6
  202.7 3.8 multiply_convert_fusion.2
  206.6 7.4 %fusion.21 = bf16[512,2304]{1,0:T(8,128)(2,1)S(1)} fusion(f32[512,2304]{1,0:T(8,128)S(1)} %get-tuple-element.74, bf16[512,1152]{1,0:T(8,128)(2,1)} %fusion.65, bf16[1152,4608]{1,0:T(8,128)(2,1)S(1)} %copy-done.58), kind=kOutput, calls=%fused_computation.41 | convolution fusion | flops 2740322304 | bytes 13565952 | tf_op jit(solution)/shard_map/td,df->tf/dot_general | solution.py:114
  214.0 9.1 %convolution_convert_fusion.1 = bf16[1152,2304]{1,0:T(8,128)(2,1)S(1)} fusion(bf16[512,2304]{1,0:T(8,128)(2,1)} %copy-done.64, bf16[512,2304]{1,0:T(8,128)(2,1)S(1)} %fusion.21, bf16[512,1152]{1,0:T(8,128)(2,1)} %collective-permute-done.3, bf16[512,1152]{1,0:T(8,128)(2,1)S(1)} %copy-done.28), kind=kOutput, calls=%fused_computation.11 | convolution fusion | flops 5452627968 | bytes 12386304 | tf_op jit(solution)/shard_map/td,tf->df/dot_general | solution.py:114
  223.2 7.9 %convolution_convert_fusion = bf16[1152,2304]{1,0:T(8,128)(2,1)S(1)} fusion(bf16[512,2304]{1,0:T(8,128)(2,1)S(1)} %copy-done.63, bf16[512,2304]{1,0:T(8,128)(2,1)S(1)} %get-tuple-element.73, bf16[512,1152]{1,0:T(8,128)(2,1)} %collective-permute-done.5, bf16[512,1152]{1,0:T(8,128)(2,1)} %fusion.65), kind=kOutput, calls=%fused_computation.10 | convolution fusion | flops 5452627968 | bytes 12386304 | tf_op jit(solution)/shard_map/td,tf->df/dot_general | solution.py:114
  231.1 4.5 pad_maximum_fusion
  235.7 8.2 %convert_add_fusion.2 = f32[512,1152]{1,0:T(8,128)} fusion(bf16[512,1152]{1,0:T(8,128)(2,1)} %collective-permute-done.6, bf16[512,2304]{1,0:T(8,128)(2,1)} %copy-done.60, bf16[1152,4608]{1,0:T(8,128)(2,1)} %all-gather.7.cloned.1.call-done), kind=kOutput, calls=%fused_computation.116 | convolution fusion | flops 2719088640 | bytes 11206656 | tf_op jit(solution)/shard_map/tf,df->td/dot_general | solution.py:114
  244.6 6.6 %fusion.40 = bf16[512,1152]{1,0:T(8,128)(2,1)S(1)} fusion(bf16[512,2304]{1,0:T(8,128)(2,1)} %get-tuple-element.75, bf16[1152,4608]{1,0:T(8,128)(2,1)} %all-gather.7.cloned.1.call-done), kind=kOutput, calls=%fused_computation.67 | convolution fusion | flops 2718498816 | bytes 8847360 | tf_op jit(solution)/shard_map/tf,df->td/dot_general | solution.py:114
  251.8 6.8 %fusion.27 = f32[512,1152]{1,0:T(8,128)S(1)} fusion(bf16[512,2304]{1,0:T(8,128)(2,1)S(1)} %copy-done.62, bf16[1152,4608]{1,0:T(8,128)(2,1)} %all-gather.7.cloned.1.call-done), kind=kOutput, calls=%fused_computation.55 | convolution fusion | flops 2717908992 | bytes 10027008 | tf_op jit(solution)/shard_map/tf,df->td/dot_general | solution.py:114
  258.7 1.6 multiply_reduce_fusion.2
  260.4 15.6 %collective-permute-done.4 = bf16[512,1152]{1,0:T(8,128)(2,1)S(1)} collective-permute-done((bf16[512,1152]{1,0:T(8,128)(2,1)S(1)}, bf16[512,1152]{1,0:T(8,128)(2,1)S(1)}, u32[]{:S(2)}, u32[]{:S(2)}) %collective-permute-start.4) | collective-permute-done | bytes 1179680 | tf_op jit(solution)/shard_map/ppermute | solution.py:88
  276.0 4.1 fusion.66
  282.2 13.3 %fusion.134 = f32[8,1024,1024]{2,1,0:T(8,128)} fusion(bf16[1024,8,72]{0,2,1:T(8,128)(2,1)S(1)} %bitcast.146, bf16[1024,8,72]{0,2,1:T(8,128)(2,1)S(1)} %bitcast.141), kind=kOutput, calls=%fused_computation.218 | convolution fusion | flops 1207959552 | bytes 35913728 | tf_op jit(solution)/shard_map/qhd,khd->hqk/dot_general | solution.py:71
  295.5 1.6 convolution_convert_fusion.11
  297.1 8.4 %collective-permute-done.7 = bf16[512,1152]{1,0:T(8,128)(2,1)S(1)} collective-permute-done((bf16[512,1152]{1,0:T(8,128)(2,1)S(1)}, bf16[512,1152]{1,0:T(8,128)(2,1)S(1)}, u32[]{:S(2)}, u32[]{:S(2)}) %collective-permute-start.7) | collective-permute-done | bytes 1179680 | tf_op jit(solution)/shard_map/ppermute | solution.py:88
  305.5 1.6 convolution_convert_fusion.10
  307.6 2.8 convolution_convert_fusion.3
  310.4 19.7 %multiply_convert_fusion = bf16[8,1024,1024]{2,1,0:T(8,128)(2,1)} fusion(f32[8,1024,1024]{2,1,0:T(8,128)} %fusion.134, f32[8,1024]{1,0:T(8,128)S(1)} %bitcast.172, f32[8,1024]{1,0:T(8,128)S(1)} %pad_maximum_fusion.7, bf16[1024,8,72]{0,2,1:T(8,128)(2,1)S(1)} %bitcast.144, bf16[1024,8,72]{0,2,1:T(8,128)(2,1)S(1)} %bitcast.150), kind=kOutput, calls=%fused_computation | convolution fusion | flops 1258291200 | bytes 52756480 | tf_op jit(solution)/shard_map/qhd,khd->hqk/dot_general | solution.py:77
  330.1 9.1 %convolution_convert_fusion.8 = bf16[8,72,1024]{2,1,0:T(8,128)(2,1)S(1)} fusion(bf16[1024,8,72]{0,2,1:T(8,128)(2,1)S(1)} %bitcast.147, bf16[8,1024,1024]{2,1,0:T(8,128)(2,1)} %multiply_convert_fusion), kind=kOutput, calls=%fused_computation.128 | convolution fusion | flops 1208549376 | bytes 19136512 | tf_op jit(solution)/shard_map/hqk,qhd->khd/dot_general | solution.py:83
  339.2 12.1 %convolution_convert_fusion.9 = bf16[8,72,1024]{2,1,0:T(8,128)(2,1)} fusion(bf16[1024,8,72]{0,2,1:T(8,128)(2,1)S(1)} %bitcast.142, bf16[8,1024,1024]{2,1,0:T(8,128)(2,1)} %multiply_convert_fusion), kind=kOutput, calls=%fused_computation.129 | convolution fusion | flops 1208549376 | bytes 19136512 | tf_op jit(solution)/shard_map/hqk,khd->qhd/dot_general | solution.py:82
  351.2 13.2 %fusion.85 = bf16[8,72,1024]{2,1,0:T(8,128)(2,1)S(1)} fusion(bf16[1024,8,72]{0,2,1:T(8,128)(2,1)S(1)} %bitcast.145, f32[8,1024,1024]{2,1,0:T(8,128)} %fusion.134, f32[8,1024]{1,0:T(8,128)} %copy-done.29), kind=kOutput, calls=%fused_computation.127 | convolution fusion | flops 1233715200 | bytes 35946496 | tf_op jit(solution)/shard_map/hqk,qhd->khd/dot_general | solution.py:74
  364.5 9.1 %convolution_convert_fusion.2 = bf16[1152,1728]{0,1:T(8,128)(2,1)S(1)} fusion(bf16[512,1152]{1,0:T(8,128)(2,1)} %copy-done.59, bf16[512,1152]{1,0:T(8,128)(2,1)} %copy-done.26, bf16[1024,576]{0,1:T(8,128)(2,1)S(1)} %bitcast.151, bf16[1024,576]{0,1:T(8,128)(2,1)S(1)} %bitcast.156, bf16[1024,576]{0,1:T(8,128)(2,1)S(1)} %bitcast.158), kind=kOutput, calls=%fused_computation.15 | convolution fusion | flops 4094189568 | bytes 9879552 | tf_op jit(solution)/shard_map/td,tc->dc/dot_general | solution.py:114
  373.6 2.8 pad_maximum_fusion.1
  376.4 2.2 convert_element_type.207
  378.7 8.6 %copy.25 = bf16[1152,2304]{1,0:T(8,128)(2,1)} copy(bf16[1152,2304]{0,1:T(8,128)(2,1)} %pad_maximum_fusion.1) | data formatting | bytes 10616832
  389.2 5.2 %convolution_convert_fusion.4 = bf16[512,1152]{1,0:T(8,128)(2,1)S(1)} fusion(bf16[1152,2304]{1,0:T(8,128)(2,1)} %all-gather.5.cloned.1.call-done, bf16[1024,1728]{0,1:T(8,128)(2,1)S(1)} %pad_maximum_fusion.2), kind=kOutput, calls=%fused_computation.68 | convolution fusion | flops 2039021568 | bytes 7077888 | tf_op jit(solution)/shard_map/tc,dc->td/dot_general | solution.py:114
  397.9 19.9 %collective-permute-done.8 = bf16[512,1152]{1,0:T(8,128)(2,1)S(1)} collective-permute-done((bf16[512,1152]{1,0:T(8,128)(2,1)S(1)}, bf16[512,1152]{1,0:T(8,128)(2,1)S(1)}, u32[]{:S(2)}, u32[]{:S(2)}) %collective-permute-start.8) | collective-permute-done | bytes 1179680 | tf_op jit(solution)/shard_map/ppermute | solution.py:88
  417.9 5.3 %fusion.63 = (f32[1152]{0:T(1024)S(1)}, f32[512]{0:T(512)}, f32[512]{0:T(512)}, f32[1152]{0:T(1024)S(1)}, f32[512,1152]{1,0:T(8,128)}) fusion(bf16[1,512,1152]{2,1,0:T(8,128)(2,1)S(1)} %copy-done.4, f32[512]{0:T(512)S(1)} %copy-done.54, f32[512]{0:T(512)S(1)} %copy-done.51, f32[1152]{0:T(1024)S(1)} %copy-done.39, ...), kind=kOutput, calls=%fused_computation.94 | convolution fusion | flops 2045506304 | bytes 10642432 | tf_op jit(solution)/shard_map/tc,dc->td/dot_general | solution.py:114
  424.4 1.4 stack.51
  425.8 1.5 reshape.147
  432.8 8.6 %all-to-all-start.1 = ((f32[16,1,432]{2,1,0:T(1,128)}), f32[16,1,432]{2,1,0:T(1,128)}, u32[]{:S(2)}, u32[]{:S(2)}) async-start(f32[16,1,432]{2,1,0:T(1,128)} %all_to_all.16), calls=%async_computation.1 | async-start | bytes 65536 | tf_op jit(solution)/shard_map/all_to_all | solution.py:231
  441.4 3.9 fusion.62
  445.3 2.8 all-to-all-done.1
  449.5 23.3 %all-gather = f32[256,576]{1,0:T(8,128)S(1)} all-gather(f32[16,576]{1,0:T(8,128)S(1)} %fusion.110), channel_id=2, replica_groups=mesh['dp'=16,'tensor'=2] {'dp'}, dimensions={0}, use_global_device_ids=true | all-gather | bytes 626688 | tf_op jit(solution)/shard_map/all_gather | solution.py:236
  472.8 2.4 fusion.108
  475.3 2.6 fusion.101
  (212 shorter events, 30.7 us)
Async XLA Ops:
  7.2 29.9 %copy-start = (bf16[1000,576]{0,1:T(8,128)(2,1)S(1)}, bf16[1000,576]{0,1:T(8,128)(2,1)}, u32[]{:S(2)}) copy-start(bf16[1000,576]{0,1:T(8,128)(2,1)} %param.13) | copy-start | bytes 3456004
  7.2 30.4 %copy-start.24 = (bf16[576,432]{0,1:T(8,128)(2,1)S(1)}, bf16[576,432]{0,1:T(8,128)(2,1)}, u32[]{:S(2)}) copy-start(bf16[576,432]{0,1:T(8,128)(2,1)} %param.14) | copy-start | bytes 1492996
  7.2 75.1 %all-gather.5.cloned.1.call-start = ((), (), s32[]{:S(2)}) async-start(), calls=%async_computation.4 | async-start | bytes 5640192 | tf_op jit(solution)/shard_map/all_gather | solution.py:135
  8.4 31.3 %copy-start.2 = (bf16[1,512,1152]{2,1,0:T(8,128)(2,1)S(1)}, bf16[1,512,1152]{2,1,0:T(8,128)(2,1)}, u32[]{:S(2)}) copy-start(bf16[1,512,1152]{2,1,0:T(8,128)(2,1)} %param.10) | copy-start | bytes 3538948
  10.3 157.8 %all-gather.7.cloned.1.call-start = ((), (), s32[]{:S(2)}) async-start(), calls=%async_computation.5 | async-start | bytes 11280384 | tf_op jit(solution)/shard_map/all_gather | solution.py:138
  38.2 3.9 collective-permute-start
  39.9 47.6 %copy-start.50 = (f32[512]{0:T(512)}, f32[512]{0:T(512)S(1)}, u32[]{:S(2)}) copy-start(f32[512]{0:T(512)S(1)} %broadcast_multiply_fusion.5) | copy-start | bytes 6148
  42.8 10.7 %all-to-all-start = ((f32[16,1,432]{2,1,0:T(1,128)}), f32[16,1,432]{2,1,0:T(1,128)S(1)}, u32[]{:S(2)}, u32[]{:S(2)}) async-start(f32[16,1,432]{2,1,0:T(1,128)} %copy.22), calls=%async_computation | async-start | bytes 65536 | tf_op jit(solution)/shard_map/all_to_all | solution.py:149
  46.3 330.2 %reduce-scatter.5.cloned.1.call-start = ((), (), s32[]{:S(2)}) async-start(), calls=%async_computation.6 | async-start | bytes 11280384 | tf_op jit(solution)/shard_map/reduce_scatter | solution.py:193
  46.3 41.2 %copy-start.53 = (f32[512]{0:T(512)}, f32[512]{0:T(512)S(1)}, u32[]{:S(2)}) copy-start(f32[512]{0:T(512)S(1)} %add_rsqrt_fusion.1) | copy-start | bytes 6148
  55.0 32.6 %copy-start.26 = (bf16[512,1152]{1,0:T(8,128)(2,1)}, bf16[512,1152]{1,0:T(8,128)(2,1)S(1)}, u32[]{:S(2)}) copy-start(bf16[512,1152]{1,0:T(8,128)(2,1)S(1)} %fusion.57) | copy-start | bytes 3538948
  55.0 27.4 %collective-permute-start.1 = (bf16[512,1152]{1,0:T(8,128)(2,1)S(1)}, bf16[512,1152]{1,0:T(8,128)(2,1)S(1)}, u32[]{:S(2)}, u32[]{:S(2)}) collective-permute-start(bf16[512,1152]{1,0:T(8,128)(2,1)S(1)} %fusion.57), channel_id=1, source_target_pairs={{0,1},{1,0},{2,3},{3,2},{4,5},{5,4},{6,7},{7,6},{8,9},{9,8},{10,11... | collective-permute-start | bytes 3538952 | tf_op jit(solution)/shard_map/ppermute | solution.py:88
  93.5 20.6 %copy-start.8 = (bf16[1024,576]{0,1:T(8,128)(2,1)}, bf16[1024,576]{0,1:T(8,128)(2,1)S(1)}, u32[]{:S(2)}) copy-start(bf16[1024,576]{0,1:T(8,128)(2,1)S(1)} %get-tuple-element.55) | copy-start | bytes 3538948
  103.2 7.3 %copy-start.22 = (bf16[8,72,512]{2,1,0:T(8,128)(2,1)}, bf16[8,72,512]{2,1,0:T(8,128)(2,1)S(1)}, u32[]{:S(2)}) copy-start(bf16[8,72,512]{2,1,0:T(8,128)(2,1)S(1)} %fusion.88) | copy-start | bytes 1769476
  106.4 26.6 %collective-permute-start.2 = (bf16[512,1152]{1,0:T(8,128)(2,1)S(1)}, bf16[512,1152]{1,0:T(8,128)(2,1)S(1)}, u32[]{:S(2)}, u32[]{:S(2)}) collective-permute-start(bf16[512,1152]{1,0:T(8,128)(2,1)S(1)} %convolution_convert_fusion.5), channel_id=1, source_target_pairs={{0,1},{1,0},{2,3},{3,2},{4,5},{5,4},{6,7},{7,6},{8,9},{9,8},{10,11... | collective-permute-start | bytes 3538952 | tf_op jit(solution)/shard_map/ppermute | solution.py:88
  114.1 18.9 %copy-start.3 = (bf16[1,512,1152]{2,1,0:T(8,128)(2,1)S(1)}, bf16[1,512,1152]{2,1,0:T(8,128)(2,1)}, u32[]{:S(2)}) copy-start(bf16[1,512,1152]{2,1,0:T(8,128)(2,1)} %param.10) | copy-start | bytes 3538948
  114.1 18.9 %copy-start.40 = (f32[1152]{0:T(1024)S(1)}, f32[1152]{0:T(1024)}, u32[]{:S(2)}) copy-start(f32[1152]{0:T(1024)} %get-tuple-element.45) | copy-start | bytes 13828
  118.2 19.7 %copy-start.13 = (bf16[8,72,512]{2,1,0:T(8,128)(2,1)}, bf16[8,72,512]{2,1,0:T(8,128)(2,1)S(1)}, u32[]{:S(2)}) copy-start(bf16[8,72,512]{2,1,0:T(8,128)(2,1)S(1)} %fusion.89) | copy-start | bytes 1769476
  139.1 29.0 %collective-permute-start.3 = (bf16[512,1152]{1,0:T(8,128)(2,1)S(1)}, bf16[512,1152]{1,0:T(8,128)(2,1)}, u32[]{:S(2)}, u32[]{:S(2)}) collective-permute-start(bf16[512,1152]{1,0:T(8,128)(2,1)S(1)} %add_convert_fusion.1), channel_id=1, source_target_pairs={{0,1},{1,0},{2,3},{3,2},{4,5},{5,4},{6,7},{7,6},{8,9},{9,8},{10,11... | collective-permute-start | bytes 3538952 | tf_op jit(solution)/shard_map/ppermute | solution.py:88
  141.9 48.4 %collective-permute-start.5 = (bf16[512,1152]{1,0:T(8,128)(2,1)}, bf16[512,1152]{1,0:T(8,128)(2,1)}, u32[]{:S(2)}, u32[]{:S(2)}) collective-permute-start(bf16[512,1152]{1,0:T(8,128)(2,1)} %fusion.65), channel_id=1, source_target_pairs={{0,1},{1,0},{2,3},{3,2},{4,5},{5,4},{6,7},{7,6},{8,9},{9,8},{10,11... | collective-permute-start | bytes 3538952 | tf_op jit(solution)/shard_map/ppermute | solution.py:88
  168.1 22.2 %copy-start.58 = (bf16[1152,4608]{1,0:T(8,128)(2,1)S(1)}, bf16[1152,4608]{1,0:T(8,128)(2,1)}, u32[]{:S(2)}) copy-start(bf16[1152,4608]{1,0:T(8,128)(2,1)} %all-gather.7.cloned.1.call-done) | copy-start | bytes 31850500
  197.0 5.8 %copy-start.28 = (bf16[512,1152]{1,0:T(8,128)(2,1)S(1)}, bf16[512,1152]{1,0:T(8,128)(2,1)}, u32[]{:S(2)}) copy-start(bf16[512,1152]{1,0:T(8,128)(2,1)} %copy-done.27) | copy-start | bytes 3538948
  201.2 34.5 %collective-permute-start.6 = (bf16[512,1152]{1,0:T(8,128)(2,1)}, bf16[512,1152]{1,0:T(8,128)(2,1)}, u32[]{:S(2)}, u32[]{:S(2)}) collective-permute-start(bf16[512,1152]{1,0:T(8,128)(2,1)} %fusion.37), channel_id=1, source_target_pairs={{0,1},{1,0},{2,3},{3,2},{4,5},{5,4},{6,7},{7,6},{8,9},{9,8},{10,11... | collective-permute-start | bytes 3538952 | tf_op jit(solution)/shard_map/ppermute | solution.py:88
  206.6 16.6 %copy-start.61 = (bf16[512,2304]{1,0:T(8,128)(2,1)}, bf16[512,2304]{1,0:T(8,128)(2,1)S(1)}, u32[]{:S(2)}) copy-start(bf16[512,2304]{1,0:T(8,128)(2,1)S(1)} %get-tuple-element.73) | copy-start | bytes 7077892
  214.0 9.2 %copy-start.60 = (bf16[512,2304]{1,0:T(8,128)(2,1)}, bf16[512,2304]{1,0:T(8,128)(2,1)S(1)}, u32[]{:S(2)}) copy-start(bf16[512,2304]{1,0:T(8,128)(2,1)S(1)} %fusion.21) | copy-start | bytes 7077892
  214.0 9.2 %copy-start.63 = (bf16[512,2304]{1,0:T(8,128)(2,1)S(1)}, bf16[512,2304]{1,0:T(8,128)(2,1)}, u32[]{:S(2)}) copy-start(bf16[512,2304]{1,0:T(8,128)(2,1)} %get-tuple-element.75) | copy-start | bytes 7077892
  243.8 235.1 %reduce-scatter.7.cloned.1.call-start = ((), (), s32[]{:S(2)}) async-start(), calls=%async_computation.7 | async-start | bytes 5640192
  244.6 65.8 %copy-start.29 = (f32[8,1024]{1,0:T(8,128)}, f32[8,1024]{1,0:T(8,128)S(1)}, u32[]{:S(2)}) copy-start(f32[8,1024]{1,0:T(8,128)S(1)} %pad_maximum_fusion.7) | copy-start | bytes 98308
  244.6 7.2 %copy-start.62 = (bf16[512,2304]{1,0:T(8,128)(2,1)S(1)}, bf16[512,2304]{1,0:T(8,128)(2,1)}, u32[]{:S(2)}) copy-start(bf16[512,2304]{1,0:T(8,128)(2,1)} %copy-done.61) | copy-start | bytes 7077892
  251.2 7.4 %copy-start.10 = (f32[512,1152]{1,0:T(8,128)S(1)}, f32[512,1152]{1,0:T(8,128)}, u32[]{:S(2)}) copy-start(f32[512,1152]{1,0:T(8,128)} %convert_add_fusion.2) | copy-start | bytes 7077892
  251.2 7.4 %copy-start.35 = (f32[1152]{0:T(1024)S(1)}, f32[1152]{0:T(1024)}, u32[]{:S(2)}) copy-start(f32[1152]{0:T(1024)} %get-tuple-element.42) | copy-start | bytes 13828
  251.2 7.4 %copy-start.43 = (f32[512]{0:T(512)S(1)}, f32[512]{0:T(512)}, u32[]{:S(2)}) copy-start(f32[512]{0:T(512)} %copy-done.42) | copy-start | bytes 6148
  251.2 7.4 %copy-start.46 = (f32[512]{0:T(512)S(1)}, f32[512]{0:T(512)}, u32[]{:S(2)}) copy-start(f32[512]{0:T(512)} %copy-done.45) | copy-start | bytes 6148
  251.3 24.7 %collective-permute-start.4 = (bf16[512,1152]{1,0:T(8,128)(2,1)S(1)}, bf16[512,1152]{1,0:T(8,128)(2,1)S(1)}, u32[]{:S(2)}, u32[]{:S(2)}) collective-permute-start(bf16[512,1152]{1,0:T(8,128)(2,1)S(1)} %fusion.40), channel_id=1, source_target_pairs={{0,1},{1,0},{2,3},{3,2},{4,5},{5,4},{6,7},{7,6},{8,9},{9,8},{10,11... | collective-permute-start | bytes 3538952 | tf_op jit(solution)/shard_map/ppermute | solution.py:88
  258.7 17.3 %copy-start.11 = (f32[512,1152]{1,0:T(8,128)S(1)}, f32[512,1152]{1,0:T(8,128)}, u32[]{:S(2)}) copy-start(f32[512,1152]{1,0:T(8,128)} %get-tuple-element.72) | copy-start | bytes 7077892
  258.7 17.2 %copy-start.16 = (bf16[512,1152]{1,0:T(8,128)(2,1)S(1)}, bf16[512,1152]{1,0:T(8,128)(2,1)}, u32[]{:S(2)}) copy-start(bf16[512,1152]{1,0:T(8,128)(2,1)} %copy-done.15) | copy-start | bytes 3538948
  258.7 17.2 %copy-start.20 = (bf16[1,512,1152]{2,1,0:T(8,128)(2,1)S(1)}, bf16[1,512,1152]{2,1,0:T(8,128)(2,1)}, u32[]{:S(2)}) copy-start(bf16[1,512,1152]{2,1,0:T(8,128)(2,1)} %param.19) | copy-start | bytes 3538948
  258.7 17.2 %copy-start.37 = (f32[1152]{0:T(1024)S(1)}, f32[1152]{0:T(1024)}, u32[]{:S(2)}) copy-start(f32[1152]{0:T(1024)} %get-tuple-element.40) | copy-start | bytes 13828
  276.0 5.5 %copy-start.41 = (f32[1152]{0:T(1024)S(1)}, f32[1152]{0:T(1024)}, u32[]{:S(2)}) copy-start(f32[1152]{0:T(1024)} %get-tuple-element.45) | copy-start | bytes 13828
  276.0 19.5 %slice-start.1 = ((s8[5308416]{0:T(1024)(128)(4,1)}), s8[4194304]{0:T(1024)(128)(4,1)S(1)}, s32[]{:S(2)}) async-start(s8[5308416]{0:T(1024)(128)(4,1)} %bitcast.166), calls=%async_computation.9 | async-start | bytes 8388608
  281.6 23.8 %collective-permute-start.7 = (bf16[512,1152]{1,0:T(8,128)(2,1)S(1)}, bf16[512,1152]{1,0:T(8,128)(2,1)S(1)}, u32[]{:S(2)}, u32[]{:S(2)}) collective-permute-start(bf16[512,1152]{1,0:T(8,128)(2,1)S(1)} %multiply_convert_fusion.3), channel_id=1, source_target_pairs={{0,1},{1,0},{2,3},{3,2},{4,5},{5,4},{6,7},{7,6},{8,9},{9,8},{10,11... | collective-permute-start | bytes 3538952 | tf_op jit(solution)/shard_map/ppermute | solution.py:88
  282.2 13.3 %slice-start.2 = ((s8[5308416]{0:T(1024)(128)(4,1)}), s8[1114112]{0:T(1024)(128)(4,1)S(1)}, s32[]{:S(2)}) async-start(s8[5308416]{0:T(1024)(128)(4,1)} %bitcast.166), calls=%async_computation.10 | async-start | bytes 2228224
  297.0 10.1 %copy-start.14 = (bf16[8,72,512]{2,1,0:T(8,128)(2,1)S(1)}, bf16[8,72,512]{2,1,0:T(8,128)(2,1)}, u32[]{:S(2)}) copy-start(bf16[8,72,512]{2,1,0:T(8,128)(2,1)} %copy-done.13) | copy-start | bytes 1769476
  297.1 10.1 %copy-start.23 = (bf16[8,72,512]{2,1,0:T(8,128)(2,1)S(1)}, bf16[8,72,512]{2,1,0:T(8,128)(2,1)}, u32[]{:S(2)}) copy-start(bf16[8,72,512]{2,1,0:T(8,128)(2,1)} %copy-done.22) | copy-start | bytes 1769476
  351.2 13.2 %copy-start.17 = (bf16[8,72,1024]{2,1,0:T(8,128)(2,1)S(1)}, bf16[8,72,1024]{2,1,0:T(8,128)(2,1)}, u32[]{:S(2)}) copy-start(bf16[8,72,1024]{2,1,0:T(8,128)(2,1)} %convolution_convert_fusion.9) | copy-start | bytes 3538948
  364.4 9.2 %copy-start.25 = (bf16[1152,576]{0,1:T(8,128)(2,1)S(1)}, bf16[1152,576]{0,1:T(8,128)(2,1)}, u32[]{:S(2)}) copy-start(bf16[1152,576]{0,1:T(8,128)(2,1)} %convolution_convert_fusion.3) | copy-start | bytes 3981316
  388.5 29.3 %slice-start.3 = ((s8[5308416]{0:T(1024)(128)(4,1)}), s8[4194304]{0:T(1024)(128)(4,1)S(1)}, s32[]{:S(2)}) async-start(s8[5308416]{0:T(1024)(128)(4,1)} %bitcast.168), calls=%async_computation.11 | async-start | bytes 8388608
  389.1 6.4 %copy-start.49 = (f32[1152]{0:T(1024)S(1)}, f32[1152]{0:T(1024)}, u32[]{:S(2)}) copy-start(f32[1152]{0:T(1024)} %get-tuple-element.32) | copy-start | bytes 13828
  389.2 7.0 %copy-start.44 = (f32[1152]{0:T(1024)S(1)}, f32[1152]{0:T(1024)}, u32[]{:S(2)}) copy-start(f32[1152]{0:T(1024)} %get-tuple-element.50) | copy-start | bytes 13828
  389.2 8.2 %copy-start.48 = (f32[1152]{0:T(1024)S(1)}, f32[1152]{0:T(1024)}, u32[]{:S(2)}) copy-start(f32[1152]{0:T(1024)} %get-tuple-element.38) | copy-start | bytes 13828
  389.2 28.6 %copy-start.4 = (bf16[1,512,1152]{2,1,0:T(8,128)(2,1)S(1)}, bf16[1,512,1152]{2,1,0:T(8,128)(2,1)}, u32[]{:S(2)}) copy-start(bf16[1,512,1152]{2,1,0:T(8,128)(2,1)} %param.10) | copy-start | bytes 3538948
  389.2 28.6 %slice-start.4 = ((s8[5308416]{0:T(1024)(128)(4,1)}), s8[1114112]{0:T(1024)(128)(4,1)S(1)}, s32[]{:S(2)}) async-start(s8[5308416]{0:T(1024)(128)(4,1)} %bitcast.168), calls=%async_computation.12 | async-start | bytes 2228224
  389.2 28.6 %copy-start.39 = (f32[1152]{0:T(1024)S(1)}, f32[1152]{0:T(1024)}, u32[]{:S(2)}) copy-start(f32[1152]{0:T(1024)} %copy-done.38) | copy-start | bytes 13828
  389.2 28.6 %copy-start.51 = (f32[512]{0:T(512)S(1)}, f32[512]{0:T(512)}, u32[]{:S(2)}) copy-start(f32[512]{0:T(512)} %copy-done.50) | copy-start | bytes 6148
  389.2 28.6 %copy-start.54 = (f32[512]{0:T(512)S(1)}, f32[512]{0:T(512)}, u32[]{:S(2)}) copy-start(f32[512]{0:T(512)} %copy-done.53) | copy-start | bytes 6148
  394.4 23.4 %collective-permute-start.8 = (bf16[512,1152]{1,0:T(8,128)(2,1)S(1)}, bf16[512,1152]{1,0:T(8,128)(2,1)S(1)}, u32[]{:S(2)}, u32[]{:S(2)}) collective-permute-start(bf16[512,1152]{1,0:T(8,128)(2,1)S(1)} %convolution_convert_fusion.4), channel_id=1, source_target_pairs={{0,1},{1,0},{2,3},{3,2},{4,5},{5,4},{6,7},{7,6},{8,9},{9,8},{10,11... | collective-permute-start | bytes 3538952 | tf_op jit(solution)/shard_map/ppermute | solution.py:88
  397.9 43.5 %copy-start.6 = (f32[512,1152]{1,0:T(8,128)S(1)}, f32[512,1152]{1,0:T(8,128)}, u32[]{:S(2)}) copy-start(f32[512,1152]{1,0:T(8,128)} %copy-done.5) | copy-start | bytes 7077892
  397.9 43.5 %copy-start.52 = (f32[512]{0:T(512)S(1)}, f32[512]{0:T(512)}, u32[]{:S(2)}) copy-start(f32[512]{0:T(512)} %copy-done.50) | copy-start | bytes 6148
  397.9 43.5 %copy-start.55 = (f32[512]{0:T(512)S(1)}, f32[512]{0:T(512)}, u32[]{:S(2)}) copy-start(f32[512]{0:T(512)} %copy-done.53) | copy-start | bytes 6148
  427.2 4.1 collective-permute-start.9
  432.8 15.3 %all-to-all-start.1 = ((f32[16,1,432]{2,1,0:T(1,128)}), f32[16,1,432]{2,1,0:T(1,128)}, u32[]{:S(2)}, u32[]{:S(2)}) async-start(f32[16,1,432]{2,1,0:T(1,128)} %all_to_all.16), calls=%async_computation.1 | async-start | bytes 65536 | tf_op jit(solution)/shard_map/all_to_all | solution.py:231
  445.3 30.0 %copy-start.31 = (f32[16,576]{1,0:T(8,128)S(1)}, f32[16,576]{1,0:T(8,128)}, u32[]{:S(2)}) copy-start(f32[16,576]{1,0:T(8,128)} %copy-done.30) | copy-start | bytes 110596
  445.3 30.0 %copy-start.57 = (s32[16]{0:T(128)S(1)}, s32[16]{0:T(128)}, u32[]{:S(2)}) copy-start(s32[16]{0:T(128)} %copy-done.56) | copy-start | bytes 196
  449.5 28.4 %copy-start.12 = (f32[72,4608]{1,0:T(8,128)S(1)}, f32[72,4608]{1,0:T(8,128)}, u32[]{:S(2)}) copy-start(f32[72,4608]{1,0:T(8,128)} %convert_element_type.207) | copy-start | bytes 3981316
  (22 other events, 57.2 us)
Sparse Core Ops, SparseCore 0:
  10.7 59.4 all-gather.4
  73.0 86.9 all-gather.6
  244.0 120.1 reduce-scatter.4
  387.4 82.3 reduce-scatter.6
